TPU v7x, 256 devices: a whole 4x4x8 slice. The times are simulated.
256 devices in a mesh: gx: 32 (over y, z_lo, x), gy: 8 (over z_hi, core).
Axes of the slice: x: 4, y: 4, z: 8 (z_hi: 4, z_lo: 2; z = z_hi * 2 + z_lo), core: 2. Of those that a mesh axis runs over, the one named last changes fastest.
Arguments:
- residual: bfloat16 [32, 8, 2048, 384], P('gx', 'gy'), may hold values from -6 to 6
- local_inverse: bfloat16 [32, 8, 2048, 2048], P('gx', 'gy'), may hold values from -0.125 to 0.125
- primal_basis: bfloat16 [32, 8, 96, 2048], P('gx', 'gy'), may hold values from -0.125 to 0.125
- row_stiffness: bfloat16 [32, 8, 2048], P('gx', 'gy'), may hold values from 0.099609375 to 10
- face_sizes: int32 [32, 8, 4], P('gx', 'gy'), may hold values from 0 to 512, as said below
- primal_slots: int32 [32, 8, 96], P('gx', 'gy'), may hold values from 0 to 287
- block_inverse: float32 [32, 8, 32, 256], P('gx', 'gy'), may hold values from -1 to 3
- level_basis: float32 [32, 8, 32, 64], P('gx', 'gy'), may hold values from -0.15625 to 0.15625
- top_inverse: float32 [64, 64], replicated, may hold values from -1 to 3
Outputs:
- preconditioned: bfloat16 [32, 8, 2048, 384], P('gx', 'gy')
Inputs may be any that keep to these rules, and one draw needn't show every extreme that they name: face_sizes[x, y, f] is equal on the two sides of a shared face, 0 on faces at the grid's edge, at least 128 elsewhere; the value 512 is reached.
All inputs are finite; a program needn't handle non-finite values.
Results may differ from a plain program's by a relative error of at most 0.008.
Values may be sent and summed in bfloat16 or wider, within the bound.
A program may use at most 64 MiB of HBM per device.

v0:
```python
import jax
import jax.numpy as jnp
from jax import lax
from jax.sharding import PartitionSpec as P


def passed_along(block, axis, distance):
    devices = range(lax.axis_size(axis))
    route = [(i - distance, i) for i in devices if i - distance in devices]
    return lax.ppermute(block, axis, route)


def extended(block, sides, width):
    for axis, dim in sides:
        count = lax.axis_size(axis)
        forward = [(i, i + 1) for i in range(count - 1)]
        backward = [(target, source) for source, target in forward]
        low = lax.ppermute(
            lax.slice_in_dim(block, block.shape[dim] - width, None, axis=dim), axis, forward
        )
        high = lax.ppermute(lax.slice_in_dim(block, 0, width, axis=dim), axis, backward)
        block = jnp.concatenate([low, block, high], axis=dim)
    return block


def coarse_lift(phi_block, values, stiffness_block):
    coarse_rows = jnp.einsum("pw,pr->wr", phi_block, values, precision=lax.Precision.HIGHEST)
    return stiffness_block[:, None] * coarse_rows


def local(
    residual,
    local_inverse,
    primal_basis,
    row_stiffness,
    face_sizes,
    primal_slots,
    block_inverse,
    level_basis,
    top_inverse,
):
    highest = lax.Precision.HIGHEST
    own_rows = residual[0, 0]
    row_count = own_rows.shape[0]
    face_rows = row_count // 4
    coarse_count = block_inverse.shape[2]
    counts = face_sizes[0, 0]
    position = jnp.arange(row_count, dtype=jnp.int32)
    face_of_row = position // face_rows
    picked = jnp.where(
        face_of_row[:, None] == jnp.arange(4, dtype=jnp.int32)[None, :], counts[None, :], 0
    )
    live_rows = position % face_rows < jnp.sum(picked, axis=1)
    masked = jnp.where(live_rows[:, None], own_rows, jnp.zeros((), jnp.bfloat16))
    local_part = jnp.dot(local_inverse[0, 0], masked, preferred_element_type=jnp.float32)
    primal_phi = primal_basis[0, 0]
    partial_value = jnp.dot(primal_phi, masked, preferred_element_type=jnp.float32)
    selector = (
        primal_slots[0, 0][:, None] == jnp.arange(9 * coarse_count, dtype=jnp.int32)[None, :]
    ).astype(jnp.float32)
    spread = jnp.einsum("ps,pr->sr", selector, partial_value, precision=highest).reshape(
        3, 3, coarse_count, -1
    )
    from_below_y = passed_along(spread[:, 2], "gy", 1)
    from_above_y = passed_along(spread[:, 0], "gy", -1)
    along_x = spread[:, 1] + from_below_y + from_above_y
    from_below_x = passed_along(along_x[2], "gx", 1)
    from_above_x = passed_along(along_x[0], "gx", -1)
    assembled = along_x[1] + from_below_x + from_above_x
    level_phi = level_basis[0, 0]
    top_rhs = lax.psum(
        jnp.einsum("cl,cr->lr", level_phi, assembled, precision=highest), ("gx", "gy")
    )
    top_value = jnp.dot(top_inverse, top_rhs, precision=highest)
    block_rhs = lax.all_gather(assembled, "gy", axis=0, tiled=True)
    coarse = jnp.dot(block_inverse[0, 0], block_rhs, precision=highest) + jnp.dot(
        level_phi, top_value, precision=highest
    )
    beside_all = extended(coarse[None, None], (("gx", 0), ("gy", 1)), 1)
    primal_values = jnp.dot(selector, beside_all.reshape(9 * coarse_count, -1), precision=highest)
    stiffness = row_stiffness[0, 0]
    stiffness_f = stiffness.astype(jnp.float32)
    phi_f = primal_phi.astype(jnp.float32)
    local_weighted = jnp.where(live_rows[:, None], stiffness_f[:, None] * local_part, 0.0)
    own_total = local_weighted + coarse_lift(phi_f, primal_values, stiffness_f)
    sent = jnp.where(live_rows[:, None], own_total, 0.0).astype(jnp.bfloat16)

    def face_parts(values):
        return [values[face_id * face_rows : (face_id + 1) * face_rows] for face_id in range(4)]

    stiff_faces = face_parts(stiffness)
    sent_faces = face_parts(sent)
    recv_low_x = passed_along((sent_faces[1], stiff_faces[1]), "gx", 1)
    recv_high_x = passed_along((sent_faces[0], stiff_faces[0]), "gx", -1)
    recv_low_y = passed_along((sent_faces[3], stiff_faces[3]), "gy", 1)
    recv_high_y = passed_along((sent_faces[2], stiff_faces[2]), "gy", -1)
    received = [recv_low_x, recv_high_x, recv_low_y, recv_high_y]
    other_sent = jnp.concatenate([item[0] for item in received], axis=0)
    other_stiffness = jnp.concatenate([item[1] for item in received], axis=0)
    summed = sent.astype(jnp.float32) + other_sent.astype(jnp.float32)
    divisor = stiffness_f + other_stiffness.astype(jnp.float32)
    result = jnp.where(live_rows[:, None], summed / divisor[:, None], 0.0).astype(jnp.bfloat16)
    return result[None, None]


def solution(mesh):
    in_specs = (
        P("gx", "gy", None, None),
        P("gx", "gy", None, None),
        P("gx", "gy", None, None),
        P("gx", "gy", None),
        P("gx", "gy", None),
        P("gx", "gy", None),
        P("gx", "gy", None, None),
        P("gx", "gy", None, None),
        P(),
    )
    out_specs = P("gx", "gy", None, None)
    return jax.shard_map(local, mesh=mesh, in_specs=in_specs, out_specs=out_specs, check_vma=False)
```

profile of v0, /device:TPU:9, one launch (start us, length us, event | category | flops | bytes accessed | tf_op | source)
XLA Modules:
  0.0 376.4 jit_solution(15713665181895772722)
XLA Ops:
  6.6 0.8 select_reduce_fusion
  7.6 2.4 fusion.7
  10.5 5.5 %collective-permute-start = (f32[3,32,384]{2,1,0:T(8,128)S(1)}, f32[3,32,384]{2,1,0:T(8,128)S(1)}, u32[]{:S(2)}, u32[]{:S(2)}) collective-permute-start(f32[3,32,384]{2,1,0:T(8,128)S(1)} %get-tuple-element.13), channel_id=1, source_target_pairs={{0,1},{1,2},{2,3},{3,4},{4,5},{5,6},{6,7},{8,9},{9,10},{10,11},{11... | collective-permute-start | bytes 442376 | tf_op jit(solution)/shard_map/ppermute | solution.py:10
  15.9 1.9 collective-permute-start.1
  18.0 6.9 %collective-permute-done.1 = f32[3,32,384]{2,1,0:T(8,128)S(1)} collective-permute-done((f32[3,32,384]{2,1,0:T(8,128)S(1)}, f32[3,32,384]{2,1,0:T(8,128)S(1)}, u32[]{:S(2)}, u32[]{:S(2)}) %collective-permute-start.1) | collective-permute-done | bytes 147488 | tf_op jit(solution)/shard_map/ppermute | solution.py:10
  24.9 3.1 collective-permute-start.2
  28.0 5.2 %collective-permute-start.3 = (f32[32,384]{1,0:T(8,128)S(1)}, f32[32,384]{1,0:T(8,128)S(1)}, u32[]{:S(2)}, u32[]{:S(2)}) collective-permute-start(f32[32,384]{1,0:T(8,128)S(1)} %get-tuple-element.16), channel_id=1, source_target_pairs={{8,0},{16,8},{24,16},{32,24},{40,32},{48,40},{56,48},{64,56},{72,6... | collective-permute-start | bytes 147464 | tf_op jit(solution)/shard_map/ppermute | solution.py:10
  33.2 1.1 collective-permute-done.3
  34.4 1.2 convolution_bitcast_fusion
  35.6 17.8 %all_gather.3 = f32[256,384]{1,0:T(8,128)S(1)} all-gather(f32[32,384]{1,0:T(8,128)S(1)} %fusion.24), channel_id=1, replica_groups=mesh['gx'=32,'gy'=8] {'gy'}, dimensions={0}, use_global_device_ids=true | all-gather | bytes 442368 | tf_op jit(solution)/shard_map/all_gather | solution.py:75
  53.4 235.0 %all-reduce.2.cloned.1.call-done = f32[64,384]{0,1:T(8,128)} async-done(((f32[64,384]{0,1:T(8,128)}), f32[64,384]{0,1:T(8,128)}) %all-reduce.2.cloned.1.call-update) | async-done | bytes 98320 | tf_op jit(solution)/shard_map/psum | solution.py:71
  288.4 1.2 fusion.38
  290.4 3.1 collective-permute-start.4
  293.5 5.2 %collective-permute-start.5 = (f32[1,1,32,384]{3,2,1,0:T(8,128)S(1)}, f32[1,1,32,384]{3,2,1,0:T(8,128)S(1)}, u32[]{:S(2)}, u32[]{:S(2)}) collective-permute-start(f32[1,1,32,384]{3,2,1,0:T(8,128)S(1)} %fusion.11), channel_id=1, source_target_pairs={{8,0},{16,8},{24,16},{32,24},{40,32},{48,40},{56,48},{64,56},{72,6... | collective-permute-start | bytes 147464 | tf_op jit(solution)/shard_map/ppermute | solution.py:21
  298.7 1.1 collective-permute-done.5
  299.9 3.7 collective-permute-start.6
  303.6 1.9 collective-permute-start.7
  305.7 6.7 %collective-permute-done.7 = f32[3,1,32,384]{3,2,1,0:T(8,128)S(1)} collective-permute-done((f32[3,1,32,384]{3,2,1,0:T(8,128)S(1)}, f32[3,1,32,384]{3,2,1,0:T(8,128)S(1)}, u32[]{:S(2)}, u32[]{:S(2)}) %collective-permute-start.7) | collective-permute-done | bytes 147488 | tf_op jit(solution)/shard_map/ppermute | solution.py:21
  312.8 1.4 fusion.12
  314.3 7.5 %fusion.4 = bf16[2048,384]{0,1:T(8,128)(2,1)S(1)} fusion(f32[384,2048]{1,0:T(8,128)S(1)} %fusion.12, bf16[1,1,2048,2048]{3,2,1,0:T(8,128)(2,1)} %param.10, f32[2048]{0:T(1024)S(1)} %bitcast.75, pred[2048]{0:T(1024)(128)(4,1)S(1)} %fusion.29, bf16[1,1,2048,384]{3,2,1,0:T(8,128)(2,1)S(1)} %copy-done.6), kind=kOutput, calls=%fused_computation.4 | convolution fusion | flops 3226730496 | bytes 14690304 | tf_op jit(solution)/shard_map/dot_general | solution.py:55
  321.9 1.9 collective-permute-start.10
  323.8 2.4 collective-permute-start.11
  326.3 2.0 collective-permute-start.8
  328.3 7.0 %collective-permute-start.9 = (bf16[512,384]{0,1:T(8,128)(2,1)S(1)}, bf16[512,384]{0,1:T(8,128)(2,1)S(1)}, u32[]{:S(2)}, u32[]{:S(2)}) collective-permute-start(bf16[512,384]{0,1:T(8,128)(2,1)S(1)} %get-tuple-element.12), channel_id=1, source_target_pairs={{8,0},{16,8},{24,16},{32,24},{40,32},{48,40},{56,48},{64,56},{72,6... | collective-permute-start | bytes 1179656 | tf_op jit(solution)/shard_map/ppermute | solution.py:10
  335.4 1.9 collective-permute-start.12
  337.3 8.3 %collective-permute-done.12 = bf16[512]{0:T(512)(128)(2,1)S(1)} collective-permute-done((bf16[512]{0:T(512)(128)(2,1)S(1)}, bf16[512]{0:T(512)(128)(2,1)S(1)}, u32[]{:S(2)}, u32[]{:S(2)}) %collective-permute-start.12) | collective-permute-done | bytes 1056 | tf_op jit(solution)/shard_map/ppermute | solution.py:10
  345.6 1.9 collective-permute-start.13
  347.5 2.4 collective-permute-done.13
  349.9 10.3 %collective-permute-start.14 = (bf16[512]{0:T(512)(128)(2,1)S(1)}, bf16[512]{0:T(512)(128)(2,1)S(1)}, u32[]{:S(2)}, u32[]{:S(2)}) collective-permute-start(bf16[512]{0:T(512)(128)(2,1)S(1)} %get-tuple-element.8), channel_id=1, source_target_pairs={{0,1},{1,2},{2,3},{3,4},{4,5},{5,6},{6,7},{8,9},{9,10},{10,11},{11... | collective-permute-start | bytes 3080 | tf_op jit(solution)/shard_map/ppermute | solution.py:10
  361.0 1.9 collective-permute-start.15
  362.9 4.4 %collective-permute-done.15 = bf16[512]{0:T(512)(128)(2,1)S(1)} collective-permute-done((bf16[512]{0:T(512)(128)(2,1)S(1)}, bf16[512]{0:T(512)(128)(2,1)S(1)}, u32[]{:S(2)}, u32[]{:S(2)}) %collective-permute-start.15) | collective-permute-done | bytes 1056 | tf_op jit(solution)/shard_map/ppermute | solution.py:10
  368.0 1.6 copy.15
  (42 shorter events, 3.7 us)
Async XLA Ops:
  6.5 1.0 copy-start
  6.5 3.4 copy-start.5
  6.5 27.8 %copy-start.1 = (f32[1,1,32,64]{3,2,1,0:T(8,128)S(1)}, f32[1,1,32,64]{3,2,1,0:T(8,128)}, u32[]{:S(2)}) copy-start(f32[1,1,32,64]{3,2,1,0:T(8,128)} %param.16) | copy-start | bytes 24580
  6.5 281.9 %all-reduce.2.cloned.1.call-start = ((), (), s32[]{:S(2)}) async-start(), calls=%async_computation | async-start | bytes 393216 | tf_op jit(solution)/shard_map/psum | solution.py:71
  7.5 280.9 %copy-start.4 = (f32[64,64]{1,0:T(8,128)S(1)}, f32[64,64]{1,0:T(8,128)}, u32[]{:S(2)}) copy-start(f32[64,64]{1,0:T(8,128)} %param.17) | copy-start | bytes 49156
  7.5 282.5 %copy-start.2 = (f32[1,1,32,256]{3,2,1,0:T(8,128)S(1)}, f32[1,1,32,256]{3,2,1,0:T(8,128)}, u32[]{:S(2)}) copy-start(f32[1,1,32,256]{3,2,1,0:T(8,128)} %param.15) | copy-start | bytes 98308
  9.9 295.6 %copy-start.3 = (bf16[1,1,2048]{2,1,0:T(2,128)(2,1)S(1)}, bf16[1,1,2048]{2,1,0:T(2,128)(2,1)}, u32[]{:S(2)}) copy-start(bf16[1,1,2048]{2,1,0:T(2,128)(2,1)} %param.12) | copy-start | bytes 12292
  10.5 7.5 %collective-permute-start = (f32[3,32,384]{2,1,0:T(8,128)S(1)}, f32[3,32,384]{2,1,0:T(8,128)S(1)}, u32[]{:S(2)}, u32[]{:S(2)}) collective-permute-start(f32[3,32,384]{2,1,0:T(8,128)S(1)} %get-tuple-element.13), channel_id=1, source_target_pairs={{0,1},{1,2},{2,3},{3,4},{4,5},{5,6},{6,7},{8,9},{9,10},{10,11},{11... | collective-permute-start | bytes 442376 | tf_op jit(solution)/shard_map/ppermute | solution.py:10
  15.9 8.9 %collective-permute-start.1 = (f32[3,32,384]{2,1,0:T(8,128)S(1)}, f32[3,32,384]{2,1,0:T(8,128)S(1)}, u32[]{:S(2)}, u32[]{:S(2)}) collective-permute-start(f32[3,32,384]{2,1,0:T(8,128)S(1)} %get-tuple-element.14), channel_id=1, source_target_pairs={{1,0},{2,1},{3,2},{4,3},{5,4},{6,5},{7,6},{9,8},{10,9},{11,10},{12... | collective-permute-start | bytes 442376 | tf_op jit(solution)/shard_map/ppermute | solution.py:10
  24.9 8.3 %collective-permute-start.2 = (f32[32,384]{1,0:T(8,128)S(1)}, f32[32,384]{1,0:T(8,128)S(1)}, u32[]{:S(2)}, u32[]{:S(2)}) collective-permute-start(f32[32,384]{1,0:T(8,128)S(1)} %get-tuple-element.15), channel_id=1, source_target_pairs={{0,8},{8,16},{16,24},{24,32},{32,40},{40,48},{48,56},{56,64},{64,7... | collective-permute-start | bytes 147464 | tf_op jit(solution)/shard_map/ppermute | solution.py:10
  28.0 6.3 %collective-permute-start.3 = (f32[32,384]{1,0:T(8,128)S(1)}, f32[32,384]{1,0:T(8,128)S(1)}, u32[]{:S(2)}, u32[]{:S(2)}) collective-permute-start(f32[32,384]{1,0:T(8,128)S(1)} %get-tuple-element.16), channel_id=1, source_target_pairs={{8,0},{16,8},{24,16},{32,24},{40,32},{48,40},{56,48},{64,56},{72,6... | collective-permute-start | bytes 147464 | tf_op jit(solution)/shard_map/ppermute | solution.py:10
  289.7 24.6 %copy-start.6 = (bf16[1,1,2048,384]{3,2,1,0:T(8,128)(2,1)S(1)}, bf16[1,1,2048,384]{3,2,1,0:T(8,128)(2,1)}, u32[]{:S(2)}) copy-start(bf16[1,1,2048,384]{3,2,1,0:T(8,128)(2,1)} %param.9) | copy-start | bytes 4718596
  290.4 8.3 %collective-permute-start.4 = (f32[1,1,32,384]{3,2,1,0:T(8,128)S(1)}, f32[1,1,32,384]{3,2,1,0:T(8,128)S(1)}, u32[]{:S(2)}, u32[]{:S(2)}) collective-permute-start(f32[1,1,32,384]{3,2,1,0:T(8,128)S(1)} %fusion.11), channel_id=1, source_target_pairs={{0,8},{8,16},{16,24},{24,32},{32,40},{40,48},{48,56},{56,64},{64,7... | collective-permute-start | bytes 147464 | tf_op jit(solution)/shard_map/ppermute | solution.py:18
  293.5 6.4 %collective-permute-start.5 = (f32[1,1,32,384]{3,2,1,0:T(8,128)S(1)}, f32[1,1,32,384]{3,2,1,0:T(8,128)S(1)}, u32[]{:S(2)}, u32[]{:S(2)}) collective-permute-start(f32[1,1,32,384]{3,2,1,0:T(8,128)S(1)} %fusion.11), channel_id=1, source_target_pairs={{8,0},{16,8},{24,16},{32,24},{40,32},{48,40},{56,48},{64,56},{72,6... | collective-permute-start | bytes 147464 | tf_op jit(solution)/shard_map/ppermute | solution.py:21
  299.9 5.9 %collective-permute-start.6 = (f32[3,1,32,384]{3,2,1,0:T(8,128)S(1)}, f32[3,1,32,384]{3,2,1,0:T(8,128)S(1)}, u32[]{:S(2)}, u32[]{:S(2)}) collective-permute-start(f32[3,1,32,384]{3,2,1,0:T(8,128)S(1)} %pad_maximum_fusion.1), channel_id=1, source_target_pairs={{0,1},{1,2},{2,3},{3,4},{4,5},{5,6},{6,7},{8,9},{9,10},{10,11},{11... | collective-permute-start | bytes 442376 | tf_op jit(solution)/shard_map/ppermute | solution.py:18
  303.6 8.8 %collective-permute-start.7 = (f32[3,1,32,384]{3,2,1,0:T(8,128)S(1)}, f32[3,1,32,384]{3,2,1,0:T(8,128)S(1)}, u32[]{:S(2)}, u32[]{:S(2)}) collective-permute-start(f32[3,1,32,384]{3,2,1,0:T(8,128)S(1)} %pad_maximum_fusion.1), channel_id=1, source_target_pairs={{1,0},{2,1},{3,2},{4,3},{5,4},{6,5},{7,6},{9,8},{10,9},{11,10},{12... | collective-permute-start | bytes 442376 | tf_op jit(solution)/shard_map/ppermute | solution.py:21
  321.9 45.4 %collective-permute-start.10 = (bf16[512,384]{0,1:T(8,128)(2,1)S(1)}, bf16[512,384]{0,1:T(8,128)(2,1)S(1)}, u32[]{:S(2)}, u32[]{:S(2)}) collective-permute-start(bf16[512,384]{0,1:T(8,128)(2,1)S(1)} %get-tuple-element.11), channel_id=1, source_target_pairs={{0,1},{1,2},{2,3},{3,4},{4,5},{5,6},{6,7},{8,9},{9,10},{10,11},{11... | collective-permute-start | bytes 1179656 | tf_op jit(solution)/shard_map/ppermute | solution.py:10
  323.8 43.5 %collective-permute-start.11 = (bf16[512,384]{0,1:T(8,128)(2,1)S(1)}, bf16[512,384]{0,1:T(8,128)(2,1)S(1)}, u32[]{:S(2)}, u32[]{:S(2)}) collective-permute-start(bf16[512,384]{0,1:T(8,128)(2,1)S(1)} %get-tuple-element.10), channel_id=1, source_target_pairs={{1,0},{2,1},{3,2},{4,3},{5,4},{6,5},{7,6},{9,8},{10,9},{11,10},{12... | collective-permute-start | bytes 1179656 | tf_op jit(solution)/shard_map/ppermute | solution.py:10
  326.3 41.1 %collective-permute-start.8 = (bf16[512,384]{0,1:T(8,128)(2,1)S(1)}, bf16[512,384]{0,1:T(8,128)(2,1)S(1)}, u32[]{:S(2)}, u32[]{:S(2)}) collective-permute-start(bf16[512,384]{0,1:T(8,128)(2,1)S(1)} %get-tuple-element.9), channel_id=1, source_target_pairs={{0,8},{8,16},{16,24},{24,32},{32,40},{40,48},{48,56},{56,64},{64,7... | collective-permute-start | bytes 1179656 | tf_op jit(solution)/shard_map/ppermute | solution.py:10
  328.3 39.0 %collective-permute-start.9 = (bf16[512,384]{0,1:T(8,128)(2,1)S(1)}, bf16[512,384]{0,1:T(8,128)(2,1)S(1)}, u32[]{:S(2)}, u32[]{:S(2)}) collective-permute-start(bf16[512,384]{0,1:T(8,128)(2,1)S(1)} %get-tuple-element.12), channel_id=1, source_target_pairs={{8,0},{16,8},{24,16},{32,24},{40,32},{48,40},{56,48},{64,56},{72,6... | collective-permute-start | bytes 1179656 | tf_op jit(solution)/shard_map/ppermute | solution.py:10
  335.4 10.2 %collective-permute-start.12 = (bf16[512]{0:T(512)(128)(2,1)S(1)}, bf16[512]{0:T(512)(128)(2,1)S(1)}, u32[]{:S(2)}, u32[]{:S(2)}) collective-permute-start(bf16[512]{0:T(512)(128)(2,1)S(1)} %get-tuple-element.5), channel_id=1, source_target_pairs={{0,8},{8,16},{16,24},{24,32},{32,40},{40,48},{48,56},{56,64},{64,7... | collective-permute-start | bytes 3080 | tf_op jit(solution)/shard_map/ppermute | solution.py:10
  345.6 4.3 %collective-permute-start.13 = (bf16[512]{0:T(512)(128)(2,1)S(1)}, bf16[512]{0:T(512)(128)(2,1)S(1)}, u32[]{:S(2)}, u32[]{:S(2)}) collective-permute-start(bf16[512]{0:T(512)(128)(2,1)S(1)} %get-tuple-element.6), channel_id=1, source_target_pairs={{8,0},{16,8},{24,16},{32,24},{40,32},{48,40},{56,48},{64,56},{72,6... | collective-permute-start | bytes 3080 | tf_op jit(solution)/shard_map/ppermute | solution.py:10
  349.9 11.1 %collective-permute-start.14 = (bf16[512]{0:T(512)(128)(2,1)S(1)}, bf16[512]{0:T(512)(128)(2,1)S(1)}, u32[]{:S(2)}, u32[]{:S(2)}) collective-permute-start(bf16[512]{0:T(512)(128)(2,1)S(1)} %get-tuple-element.8), channel_id=1, source_target_pairs={{0,1},{1,2},{2,3},{3,4},{4,5},{5,6},{6,7},{8,9},{9,10},{10,11},{11... | collective-permute-start | bytes 3080 | tf_op jit(solution)/shard_map/ppermute | solution.py:10
  361.0 6.3 %collective-permute-start.15 = (bf16[512]{0:T(512)(128)(2,1)S(1)}, bf16[512]{0:T(512)(128)(2,1)S(1)}, u32[]{:S(2)}, u32[]{:S(2)}) collective-permute-start(bf16[512]{0:T(512)(128)(2,1)S(1)} %get-tuple-element.7), channel_id=1, source_target_pairs={{1,0},{2,1},{3,2},{4,3},{5,4},{6,5},{7,6},{9,8},{10,9},{11,10},{12... | collective-permute-start | bytes 3080 | tf_op jit(solution)/shard_map/ppermute | solution.py:10
Sparse Core Ops, SparseCore 0:
  35.7 252.6 all-reduce.1
where the time goes:
time: 377 us; the launch traced here: 376 us
  waiting for transfers between devices  267 us (71%)
  starting transfers between devices  59.1 us (16%)
  blocking collectives  17.8 us (5%)
  matrix products  15.3 us (4%)
  between operations  13.8 us (4%)
    psum x1, waiting for transfers between devices, local(): lax.psum(jnp.einsum('cl,cr->lr', level_phi, assembled, precision=highest)...  235 us
    ppermute x12, starting transfers between devices, passed_along(): return lax.ppermute(block, axis, route)  45.2 us
    ppermute x12, waiting for transfers between devices, passed_along(): return lax.ppermute(block, axis, route)  24 us
    all_gather x1, blocking collectives, local(): block_rhs = lax.all_gather(assembled, 'gy', axis=0, tiled=True)  17.8 us
    ppermute x2, waiting for transfers between devices, extended(): lax.ppermute(lax.slice_in_dim(block, 0, width, axis=dim), axis, backward)  7.81 us
  transfers between devices with their start and end apart: 17, of which 11 were waited for; matrix products, arithmetic and copies ran while one was open for 0% of the time, Pallas kernels for 0%

commit v1 on v0

v1 whole, which is shorter than its diff:
```python
import functools

import jax
import jax.numpy as jnp
from jax import lax
from jax.experimental import pallas as pl
from jax.experimental.pallas import tpu as pltpu
from jax.sharding import PartitionSpec as P

MESH = pl.DeviceIdType.MESH
HIGHEST = lax.Precision.HIGHEST
F32 = jnp.float32
BF16 = jnp.bfloat16
RUN = 4
OFFSETS = [(a, b) for a in (-1, 0, 1) for b in (-1, 0, 1) if (a, b) != (0, 0)]
FACES = [(-1, 0), (1, 0), (0, -1), (0, 1)]
TILE = 256


def dot(a, b, dims=((1,), (0,)), precision=None):
    return lax.dot_general(a, b, (dims, ((), ())), preferred_element_type=F32, precision=precision)


def slot_of(a, b):
    return (a + 1) * 3 + (b + 1)


def apply_kernel(
    gx_count,
    gy_count,
    res_h, inv_h, phi_h, stiff_h, sizes_h, slots_h, block_h, level_h, topinv_h,
    acc_h, w_h, top_h,
    res, inv, phi, stiff, sizes, slots, block, level, topinv,
    masked, col, dencol, lev_ext, partial, part_send, part_recv, asm, blk, coarse_ext,
    stat_send, stat_recv, bulk_send, bulk_recv, low_send, low_recv,
    red_send, red_recv, run_send, run_recv, far_send, far_recv, piece_send, top,
    acc, wt,
    load_sem, inv_sem, out_sem,
    lev_s, lev_r, part_s, part_r, coarse_s, coarse_r,
    stat_s, stat_r, bulk_s, bulk_r, low_s, low_r,
    red_s, red_r, asm_s, asm_r, run_s, run_r, far_s, far_r, top_s, top_r,
):
    x = lax.axis_index("gx")
    y = lax.axis_index("gy")
    rows, width = res.shape
    face = rows // 4
    primal = phi.shape[0]
    cdev, top_size = level.shape
    far_count = gx_count // RUN
    piece = top_size // gy_count
    pending = []

    def inside(a, b):
        ok_x = jnp.logical_and(x + a >= 0, x + a < gx_count)
        ok_y = jnp.logical_and(y + b >= 0, y + b < gy_count)
        return jnp.logical_and(ok_x, ok_y)

    def remote(src, dst, send, recv, dev):
        return pltpu.make_async_remote_copy(
            src_ref=src, dst_ref=dst, send_sem=send, recv_sem=recv,
            device_id=dev, device_id_type=MESH)

    def beside(a, b, src, dst, send, recv):
        @pl.when(inside(a, b))
        def _():
            remote(src, dst, send, recv, (x + a, y + b)).start()

        def done():
            @pl.when(inside(a, b))
            def _():
                remote(src, dst, send, recv, (x + a, y + b)).wait_send()
        pending.append(done)

    def arrived(a, b, dst, send, recv):
        @pl.when(inside(a, b))
        def _():
            remote(dst, dst, send, recv, (x + a, y + b)).wait_recv()

    def zero_outside(a, b, ref):
        @pl.when(jnp.logical_not(inside(a, b)))
        def _():
            ref[...] = jnp.zeros(ref.shape, ref.dtype)

    def gy_peer(d):
        return (x, lax.rem(y + d, gy_count))

    def run_peer(d):
        return (x - lax.rem(x, RUN) + lax.rem(lax.rem(x, RUN) + d, RUN), y)

    def far_peer(d):
        return (lax.rem(x // RUN + d, far_count) * RUN + lax.rem(x, RUN), y)

    def to_group(peer, d, src, dst, send, recv):
        remote(src, dst, send.at[d], recv.at[d], peer(d)).start()
        pending.append(lambda: remote(src, dst, send.at[d], recv.at[d], peer(d)).wait_send())

    def group_arrived(peer, d, dst, send, recv):
        remote(dst, dst, send.at[d], recv.at[d], peer(d)).wait_recv()

    loads = [
        pltpu.make_async_copy(src, dst, load_sem.at[i])
        for i, (src, dst) in enumerate([
            (level_h, level), (slots_h, slots), (sizes_h, sizes), (stiff_h, stiff),
            (topinv_h, topinv), (block_h, block), (phi_h, phi)])
    ]
    res_loads = [
        pltpu.make_async_copy(
            res_h.at[pl.ds(f * face, face)], res.at[pl.ds(f * face, face)],
            load_sem.at[len(loads) + f])
        for f in range(4)
    ]
    inv_loads = [
        pltpu.make_async_copy(
            inv_h.at[pl.ds(f * face, face)], inv.at[pl.ds(f * face, face)], inv_sem.at[f])
        for f in range(4)
    ]
    for copy in loads + res_loads + inv_loads:
        copy.start()
    barrier = pltpu.get_barrier_semaphore()
    for a, b in OFFSETS:
        @pl.when(inside(a, b))
        def _():
            pl.semaphore_signal(barrier, inc=1, device_id=(x + a, y + b), device_id_type=MESH)
    for peer, count in ((gy_peer, gy_count), (run_peer, RUN), (far_peer, far_count)):
        for d in range(1, count):
            pl.semaphore_signal(barrier, inc=1, device_id=peer(d), device_id_type=MESH)

    for a, b in OFFSETS:
        zero_outside(a, b, lev_ext.at[slot_of(a, b)])
        zero_outside(a, b, part_recv.at[slot_of(a, b)])
        zero_outside(a, b, coarse_ext.at[slot_of(a, b)])
    for f, (a, b) in enumerate(FACES):
        zero_outside(a, b, stat_recv.at[f])
        zero_outside(a, b, bulk_recv.at[f])
        zero_outside(a, b, low_recv.at[f])

    for copy in loads:
        copy.wait()
    slot_row = jnp.broadcast_to(slots[...], (9 * cdev, primal))
    slot_iota = lax.broadcasted_iota(jnp.int32, (9 * cdev, primal), 0)
    sel_t = jnp.where(slot_row == slot_iota, 1.0, 0.0).astype(F32)
    sel_t16 = sel_t.astype(BF16)
    lev_ext[slot_of(0, 0)] = level[...]

    def one(flag):
        return jnp.where(flag, 1, 0)

    count_x = 1 + one(x > 0) + one(x < gx_count - 1)
    count_y = 1 + one(y > 0) + one(y < gy_count - 1)
    pl.semaphore_wait(
        barrier, count_x * count_y - 1 + gy_count - 1 + RUN - 1 + far_count - 1)

    for i, (a, b) in enumerate(OFFSETS):
        beside(a, b, level, lev_ext.at[slot_of(-a, -b)], lev_s.at[i], lev_r.at[slot_of(-a, -b)])

    for f in range(4):
        res_loads[f].wait()
        live = lax.broadcasted_iota(jnp.int32, (face, width), 0) < sizes[0, f]
        part = res[pl.ds(f * face, face), :].astype(F32)
        masked[pl.ds(f * face, face), :] = jnp.where(live, part, 0.0).astype(BF16)
    partial[...] = dot(phi[...], masked[...])
    spread = dot(sel_t16, partial[...].astype(BF16))
    for k in range(9):
        part_send[k] = spread[k * cdev:(k + 1) * cdev].astype(BF16)
    for i, (a, b) in enumerate(OFFSETS):
        beside(a, b, part_send.at[slot_of(a, b)], part_recv.at[slot_of(-a, -b)],
               part_s.at[i], part_r.at[slot_of(-a, -b)])

    stiff32 = stiff[...].astype(F32)
    for f, (a, b) in enumerate(FACES):
        stat_send[f, :primal, :] = phi[:, f * face:(f + 1) * face]
        stat_send[f, primal:, :] = jnp.broadcast_to(
            stiff32[:, f * face:(f + 1) * face], (16, face)).astype(BF16)
        beside(a, b, stat_send.at[f], stat_recv.at[f ^ 1], stat_s.at[f], stat_r.at[f ^ 1])

    for a, b in OFFSETS:
        arrived(a, b, lev_ext.at[slot_of(a, b)], lev_s.at[0], lev_r.at[slot_of(a, b)])
    lev_all = lev_ext[...].reshape(9 * cdev, top_size)
    basis = dot(sel_t, lev_all, ((0,), (0,)), HIGHEST)
    basis_inv = dot(basis, topinv[...], ((1,), (1,)), HIGHEST)
    red_send[...] = dot(basis_inv, partial[...], ((0,), (0,)), HIGHEST)

    def piece_rows(index):
        return pl.ds(pl.multiple_of(index * piece, piece), piece)

    for d in range(1, gy_count):
        to_group(gy_peer, d, red_send.at[piece_rows(lax.rem(y + d, gy_count))],
                 red_recv.at[d], red_s, red_r)

    total = part_send[slot_of(0, 0)].astype(F32)
    for a, b in OFFSETS:
        arrived(a, b, part_recv.at[slot_of(a, b)], part_s.at[0], part_r.at[slot_of(a, b)])
        total = total + part_recv[slot_of(a, b)].astype(F32)
    asm[...] = total.astype(BF16)
    own_rows = pl.ds(pl.multiple_of(y * cdev, cdev), cdev)
    for d in range(1, gy_count):
        to_group(gy_peer, d, asm, blk.at[own_rows], asm_s, asm_r)
    blk[own_rows, :] = total.astype(BF16)

    for f in range(4):
        lane = lax.broadcasted_iota(jnp.int32, (1, face), 1)
        weight = jnp.where(lane < sizes[0, f], stiff32[:, f * face:(f + 1) * face], 0.0)
        for j in range(face // 128):
            square = jnp.broadcast_to(weight[:, j * 128:(j + 1) * 128], (128, 128))
            col[pl.ds(f * face + j * 128, 128), :] = square.T

    tile = min(TILE, face)

    def across(column):
        return jnp.concatenate([column] * (width // 128), axis=1)

    def local_face(f):
        inv_loads[f].wait()

        def step(i, carry):
            first = pl.multiple_of(f * face + i * tile, tile)
            value = dot(inv[pl.ds(first, tile), :], masked[...])
            value = value * across(col[pl.ds(first, tile), :])
            bulk_send[f, pl.ds(pl.multiple_of(i * tile, tile), tile), :] = value.astype(BF16)
            return carry

        lax.fori_loop(0, face // tile, step, 0)
        a, b = FACES[f]
        beside(a, b, bulk_send.at[f], bulk_recv.at[f ^ 1], bulk_s.at[f], bulk_r.at[f ^ 1])

    local_face(0)
    local_face(1)

    total = red_send[piece_rows(y), :]
    for d in range(1, gy_count):
        group_arrived(gy_peer, d, red_recv.at[d], red_s, red_r)
        total = total + red_recv[d]
    run_send[...] = total
    for d in range(1, RUN):
        to_group(run_peer, d, run_send, run_recv.at[d], run_s, run_r)
    local_face(2)
    total = run_send[...]
    for d in range(1, RUN):
        group_arrived(run_peer, d, run_recv.at[d], run_s, run_r)
        total = total + run_recv[d]
    far_send[...] = total
    for d in range(1, far_count):
        to_group(far_peer, d, far_send, far_recv.at[d], far_s, far_r)

    for d in range(1, gy_count):
        group_arrived(gy_peer, d, asm, asm_s, asm_r)
    coarse = dot(block[...], blk[...].astype(F32), precision=HIGHEST)
    coarse_ext[slot_of(0, 0)] = coarse.astype(BF16)
    for i, (a, b) in enumerate(OFFSETS):
        beside(a, b, coarse_ext.at[slot_of(0, 0)], coarse_ext.at[slot_of(-a, -b)],
               coarse_s.at[i], coarse_r.at[slot_of(-a, -b)])
    local_face(3)

    total = far_send[...]
    for d in range(1, far_count):
        group_arrived(far_peer, d, far_recv.at[d], far_s, far_r)
        total = total + far_recv[d]
    piece_send[...] = total
    for d in range(1, gy_count):
        to_group(gy_peer, d, piece_send, top.at[piece_rows(y)], top_s, top_r)
    top[piece_rows(y), :] = total

    for a, b in OFFSETS:
        arrived(a, b, coarse_ext.at[slot_of(a, b)], coarse_s.at[0], coarse_r.at[slot_of(a, b)])
    ext = coarse_ext[...].reshape(9 * cdev, width)
    low_send[:, :width] = dot(sel_t16, ext, ((0,), (0,))).astype(BF16)
    low_send[:, width:] = jnp.concatenate(
        [basis, jnp.zeros((primal, low_send.shape[1] - width - top_size), F32)], axis=1
    ).astype(BF16)
    for f, (a, b) in enumerate(FACES):
        beside(a, b, low_send, low_recv.at[f ^ 1], low_s.at[f], low_r.at[f ^ 1])

    outs = []
    for f, (a, b) in enumerate(FACES):
        arrived(a, b, stat_recv.at[f], stat_s.at[f], stat_r.at[f])
        lane = lax.broadcasted_iota(jnp.int32, (1, face), 1)
        live = lane < sizes[0, f]
        own = stiff32[:, f * face:(f + 1) * face]
        other = stat_recv[f, primal:primal + 8, :].astype(F32)[:1]
        scale = jnp.where(live, 1.0 / (own + other), 0.0)
        for j in range(face // 128):
            square = jnp.broadcast_to(scale[:, j * 128:(j + 1) * 128], (128, 128))
            dencol[pl.ds(f * face + j * 128, 128), :] = square.T
        own_phi = (stat_send[f, :primal, :].astype(F32) * (own * scale)).astype(BF16)
        other_phi = (stat_recv[f, :primal, :].astype(F32) * (other * scale)).astype(BF16)
        arrived(a, b, low_recv.at[f], low_s.at[f], low_r.at[f])
        both = dot(own_phi, low_send[...], ((0,), (0,))) + dot(other_phi, low_recv[f], ((0,), (0,)))
        arrived(a, b, bulk_recv.at[f], bulk_s.at[f], bulk_r.at[f])
        here = pl.ds(f * face, face)
        summed = bulk_send[f].astype(F32) + bulk_recv[f].astype(F32)
        acc[here, :] = both[:, :width] + summed * across(dencol[here, :])
        wt[here, :] = both[:, width:].astype(BF16)
        for k, (src, dst) in enumerate(((acc, acc_h), (wt, w_h))):
            copy = pltpu.make_async_copy(src.at[here], dst.at[here], out_sem.at[2 * f + k])
            copy.start()
            outs.append(copy)

    for d in range(1, gy_count):
        group_arrived(gy_peer, d, top.at[piece_rows(0)], top_s, top_r)
    copy = pltpu.make_async_copy(top, top_h, out_sem.at[8])
    copy.start()
    outs.append(copy)
    for copy in outs:
        copy.wait()
    for done in pending:
        done()


def finish_kernel(acc, wt, top, out):
    value = dot(wt[:, :top.shape[0]], top[...].astype(BF16))
    out[...] = (acc[...] + value).astype(BF16)


def local(gx_count, gy_count, residual, local_inverse, primal_basis, row_stiffness,
          face_sizes, primal_slots, block_inverse, level_basis, top_inverse):
    rows, width = residual.shape[2:]
    face = rows // 4
    primal = primal_basis.shape[2]
    cdev, top_size = level_basis.shape[2:]
    block_size = block_inverse.shape[3]
    far_count = gx_count // RUN
    piece = top_size // gy_count
    low_width = width + 128
    vm = pltpu.VMEM
    dma = pltpu.SemaphoreType.DMA
    args = (residual[0, 0], local_inverse[0, 0], primal_basis[0, 0], row_stiffness[0],
            face_sizes[0], primal_slots[0], block_inverse[0, 0], level_basis[0, 0], top_inverse)
    halo = dma((9,))
    four = dma((4,))
    gys = dma((gy_count,))
    scratch = [
        vm((rows, width), BF16), vm((rows, rows), BF16), vm((primal, rows), BF16),
        vm((1, rows), BF16), pltpu.SMEM((1, 4), jnp.int32), vm((1, primal), jnp.int32),
        vm((cdev, block_size), F32), vm((cdev, top_size), F32), vm((top_size, top_size), F32),
        vm((rows, width), BF16), vm((rows, 128), F32), vm((rows, 128), F32),
        vm((9, cdev, top_size), F32), vm((primal, width), F32),
        vm((9, cdev, width), BF16), vm((9, cdev, width), BF16),
        vm((cdev, width), BF16), vm((block_size, width), BF16), vm((9, cdev, width), BF16),
        vm((4, primal + 16, face), BF16), vm((4, primal + 16, face), BF16),
        vm((4, face, width), BF16), vm((4, face, width), BF16),
        vm((primal, low_width), BF16), vm((4, primal, low_width), BF16),
        vm((top_size, width), F32), vm((gy_count, piece, width), F32),
        vm((piece, width), F32), vm((RUN, piece, width), F32),
        vm((piece, width), F32), vm((far_count, piece, width), F32),
        vm((piece, width), F32), vm((top_size, width), F32),
        vm((rows, width), F32), vm((rows, 128), BF16),
        dma((11,)), four, dma((9,)),
        halo, halo, halo, halo, halo, halo,
        four, four, four, four, four, four,
        gys, gys, gys, gys, dma((RUN,)), dma((RUN,)), dma((far_count,)), dma((far_count,)),
        gys, gys,
    ]
    acc, wt, top = pl.pallas_call(
        functools.partial(apply_kernel, gx_count, gy_count),
        name="apply",
        out_shape=(
            jax.ShapeDtypeStruct((rows, width), F32),
            jax.ShapeDtypeStruct((rows, 128), BF16),
            jax.ShapeDtypeStruct((top_size, width), F32),
        ),
        in_specs=[pl.BlockSpec(memory_space=pl.ANY)] * len(args),
        out_specs=[pl.BlockSpec(memory_space=pl.ANY)] * 3,
        scratch_shapes=scratch,
        compiler_params=pltpu.CompilerParams(
            collective_id=0, has_side_effects=True, vmem_limit_bytes=56 << 20),
    )(*args)
    out = pl.pallas_call(
        finish_kernel,
        name="finish",
        grid=(4,),
        out_shape=jax.ShapeDtypeStruct((rows, width), BF16),
        in_specs=[
            pl.BlockSpec((face, width), lambda i: (i, 0)),
            pl.BlockSpec((face, 128), lambda i: (i, 0)),
            pl.BlockSpec((top_size, width), lambda i: (0, 0)),
        ],
        out_specs=pl.BlockSpec((face, width), lambda i: (i, 0)),
    )(acc, wt, top)
    return out[None, None]


def solution(mesh):
    in_specs = (
        P("gx", "gy", None, None),
        P("gx", "gy", None, None),
        P("gx", "gy", None, None),
        P("gx", "gy", None),
        P("gx", "gy", None),
        P("gx", "gy", None),
        P("gx", "gy", None, None),
        P("gx", "gy", None, None),
        P(),
    )
    out_specs = P("gx", "gy", None, None)
    body = functools.partial(local, mesh.shape["gx"], mesh.shape["gy"])
    return jax.shard_map(body, mesh=mesh, in_specs=in_specs, out_specs=out_specs, check_vma=False)
```

time: 377 us -> 64.4 us (0.17)
  the two profiles are of different devices: /device:TPU:9 before, /device:TPU:1 now
where the time goes in v1:
time: 64.4 us; the launch traced here: 63.1 us
  Pallas kernels  63.1 us (98%)
    pallas_call x1, Pallas kernels, local(): pl.pallas_call(functools.partial(apply_kernel, gx_count, gy_count), name=...  58.5 us
    pallas_call x1, Pallas kernels, local(): pl.pallas_call(finish_kernel, name='finish', grid=(4,), out_shape=jax.Sha...  4.6 us

profile of v1, /device:TPU:1, one launch (start us, length us, event | category | flops | bytes accessed | tf_op | source)
XLA Modules:
  0.0 63.1 jit_solution(8010974042701526729)
XLA Ops:
  0.0 58.5 %apply.1 = (f32[2048,384]{1,0:T(8,128)}, bf16[2048,128]{1,0:T(8,128)(2,1)}, f32[64,384]{1,0:T(8,128)}) custom-call(bf16[2048,384]{1,0:T(8,128)(2,1)} %bitcast.10, bf16[2048,2048]{1,0:T(8,128)(2,1)} %bitcast.9, bf16[96,2048]{1,0:T(8,128)(2,1)} %bitcast.11, bf16[1,2048]{1,0:T(2,128)(2,1)} %bitcast.14, s32[1,4]{1,0:T(1,128)} %bitcast.15, s32[1,96]{1,0:T(1,128)} %bitcast.16, ...), custom_call_target="tpu_custom_call" | custom-call | tf_op jit(solution)/shard_map/apply/pallas_call | solution.py:353
  58.5 4.6 %finish.1 = bf16[2048,384]{1,0:T(8,128)(2,1)} custom-call(f32[2048,384]{1,0:T(8,128)} %get-tuple-element.8.acc, bf16[2048,128]{1,0:T(8,128)(2,1)} %get-tuple-element.9.wt, f32[64,384]{1,0:T(8,128)} %get-tuple-element.10.top), custom_call_target="tpu_custom_call" | custom-call | tf_op jit(solution)/shard_map/finish/pallas_call | solution.py:367

commit v2 on v1

v2 whole, which is shorter than its diff:
```python
import functools

import jax
import jax.numpy as jnp
from jax import lax
from jax.experimental import pallas as pl
from jax.experimental.pallas import tpu as pltpu
from jax.sharding import PartitionSpec as P

MESH = pl.DeviceIdType.MESH
HIGHEST = lax.Precision.HIGHEST
F32 = jnp.float32
BF16 = jnp.bfloat16
RUN = 4
OFFSETS = [(a, b) for a in (-1, 0, 1) for b in (-1, 0, 1) if (a, b) != (0, 0)]
FACES = [(-1, 0), (1, 0), (0, -1), (0, 1)]


def dot(a, b, dims=((1,), (0,)), precision=None):
    return lax.dot_general(a, b, (dims, ((), ())), preferred_element_type=F32, precision=precision)


def slot_of(a, b):
    return (a + 1) * 3 + (b + 1)


def apply_kernel(
    gx_count,
    gy_count,
    res_h, inv_h, phi_h, stiff_h, sizes_h, slots_h, block_h, level_h, topinv_h,
    acc, phit, low_out, lowr_out, top_out,
    res, inv, phi, stiff, sizes, slots, block, level, topinv,
    masked, col, dencol, lev_ext, partial, part_send, part_recv, asm, blk, coarse_ext,
    stat_send, stat_recv, bulk_send, bulk_recv, low_send, low_recv,
    red_send, red_recv, run_send, run_recv, far_send, far_recv, piece_send, top,
    via_bulk, via_stat, load_sem, inv_sem,
    lev_s, lev_r, part_s, part_r, coarse_s, coarse_r,
    stat_s, stat_r, bulk_s, bulk_r, low_s, low_r,
    via_s, via_r, red_s, red_r, asm_s, asm_r, run_s, run_r, far_s, far_r, top_s, top_r,
):
    x = lax.axis_index("gx")
    y = lax.axis_index("gy")
    rows, width = res.shape
    face = rows // 4
    primal = phi.shape[0]
    cdev, top_size = level.shape
    far_count = gx_count // RUN
    piece = top_size // gy_count
    pending = []

    def inside(a, b):
        ok_x = jnp.logical_and(x + a >= 0, x + a < gx_count)
        ok_y = jnp.logical_and(y + b >= 0, y + b < gy_count)
        return jnp.logical_and(ok_x, ok_y)

    def remote(src, dst, send, recv, dev):
        return pltpu.make_async_remote_copy(
            src_ref=src, dst_ref=dst, send_sem=send, recv_sem=recv,
            device_id=dev, device_id_type=MESH)

    def beside(a, b, src, dst, send, recv):
        @pl.when(inside(a, b))
        def _():
            remote(src, dst, send, recv, (x + a, y + b)).start()

        def done():
            @pl.when(inside(a, b))
            def _():
                remote(src, dst, send, recv, (x + a, y + b)).wait_send()
        pending.append(done)

    def arrived(a, b, dst, send, recv):
        @pl.when(inside(a, b))
        def _():
            remote(dst, dst, send, recv, (x + a, y + b)).wait_recv()

    def zero_outside(a, b, ref):
        @pl.when(jnp.logical_not(inside(a, b)))
        def _():
            ref[...] = jnp.zeros(ref.shape, ref.dtype)

    place = lax.rem(x, RUN)
    hop = jnp.where(place >= RUN // 2, 2, -2)
    third = x + hop
    has_third = jnp.logical_and(third >= 0, third < gx_count)
    passes_low = jnp.logical_and(place == 2, has_third)
    passes_high = jnp.logical_and(place == 1, has_third)

    def to_face(f, src, dst, send, recv, via, via_recv):
        a, b = FACES[f]
        if f > 1:
            beside(a, b, src, dst, send, recv)
            return
        last = place == (RUN - 1 if f == 1 else 0)
        ok = inside(a, b)

        @pl.when(jnp.logical_and(ok, jnp.logical_not(last)))
        def _():
            remote(src, dst, send, recv, (x + a, y)).start()

        @pl.when(jnp.logical_and(ok, last))
        def _():
            remote(src, via, send, via_recv, (x - a, y)).start()

        def done():
            @pl.when(ok)
            def _():
                remote(src, dst, send, recv, (x + a, y)).wait_send()
        pending.append(done)

    def pass_on(via, k, dst, recv):
        for slot, flag, a in ((0, passes_low, 2), (1, passes_high, -2)):
            @pl.when(flag)
            def _():
                remote(via, via, via_s.at[k], via_r.at[k], (x + a, y)).wait_recv()
                remote(via, dst(slot), via_s.at[k], recv(slot), (x + a, y)).start()

            def done(slot=slot, flag=flag, a=a):
                @pl.when(flag)
                def _():
                    remote(via, dst(slot), via_s.at[k], recv(slot), (x + a, y)).wait_send()
            pending.append(done)

    def gy_peer(d):
        return (x, lax.rem(y + d, gy_count))

    def run_peer(d):
        return (x - lax.rem(x, RUN) + lax.rem(lax.rem(x, RUN) + d, RUN), y)

    def far_peer(d):
        return (lax.rem(x // RUN + d, far_count) * RUN + lax.rem(x, RUN), y)

    def to_group(peer, d, src, dst, send, recv):
        remote(src, dst, send.at[d], recv.at[d], peer(d)).start()
        pending.append(lambda: remote(src, dst, send.at[d], recv.at[d], peer(d)).wait_send())

    def group_arrived(peer, d, dst, send, recv):
        remote(dst, dst, send.at[d], recv.at[d], peer(d)).wait_recv()

    loads = [
        pltpu.make_async_copy(src, dst, load_sem.at[i])
        for i, (src, dst) in enumerate([
            (level_h, level), (slots_h, slots), (sizes_h, sizes), (stiff_h, stiff),
            (topinv_h, topinv), (block_h, block), (phi_h, phi)])
    ]
    res_loads = [
        pltpu.make_async_copy(
            res_h.at[pl.ds(f * face, face)], res.at[pl.ds(f * face, face)],
            load_sem.at[len(loads) + f])
        for f in range(4)
    ]
    quarter = face // 4

    def quarter_rows(f, q):
        return pl.ds(f * face + q * quarter, quarter)

    inv_loads = [
        pltpu.make_async_copy(
            inv_h.at[quarter_rows(f, q)], inv.at[quarter_rows(f, q)], inv_sem.at[4 * q + f])
        for q in range(4) for f in range(4)
    ]
    for copy in loads + res_loads + inv_loads:
        copy.start()
    barrier = pltpu.get_barrier_semaphore()
    for a, b in OFFSETS:
        @pl.when(inside(a, b))
        def _():
            pl.semaphore_signal(barrier, inc=1, device_id=(x + a, y + b), device_id_type=MESH)
    @pl.when(has_third)
    def _():
        pl.semaphore_signal(barrier, inc=1, device_id=(third, y), device_id_type=MESH)
    for peer, count in ((gy_peer, gy_count), (run_peer, RUN), (far_peer, far_count)):
        for d in range(1, count):
            pl.semaphore_signal(barrier, inc=1, device_id=peer(d), device_id_type=MESH)

    for a, b in OFFSETS:
        zero_outside(a, b, lev_ext.at[slot_of(a, b)])
        zero_outside(a, b, part_recv.at[slot_of(a, b)])
        zero_outside(a, b, coarse_ext.at[slot_of(a, b)])
    for f, (a, b) in enumerate(FACES):
        zero_outside(a, b, stat_recv.at[f])
        zero_outside(a, b, bulk_recv.at[f])
        zero_outside(a, b, low_recv.at[f])

    for copy in loads:
        copy.wait()
    slot_row = jnp.broadcast_to(slots[...], (9 * cdev, primal))
    slot_iota = lax.broadcasted_iota(jnp.int32, (9 * cdev, primal), 0)
    sel_t = jnp.where(slot_row == slot_iota, 1.0, 0.0).astype(F32)
    sel_t16 = sel_t.astype(BF16)
    lev_ext[slot_of(0, 0)] = level[...]

    for f in range(4):
        res_loads[f].wait()
        live = lax.broadcasted_iota(jnp.int32, (face, width), 0) < sizes[0, f]
        part = res[pl.ds(f * face, face), :].astype(F32)
        masked[pl.ds(f * face, face), :] = jnp.where(live, part, 0.0).astype(BF16)
    partial[...] = dot(phi[...], masked[...])
    spread = dot(sel_t16, partial[...].astype(BF16))
    for k in range(9):
        part_send[k] = spread[k * cdev:(k + 1) * cdev].astype(BF16)
    def one(flag):
        return jnp.where(flag, 1, 0)

    count_x = 1 + one(x > 0) + one(x < gx_count - 1)
    count_y = 1 + one(y > 0) + one(y < gy_count - 1)
    pl.semaphore_wait(
        barrier, count_x * count_y - 1 + one(has_third) + gy_count - 1 + RUN - 1 + far_count - 1)

    for i, (a, b) in enumerate(OFFSETS):
        beside(a, b, level, lev_ext.at[slot_of(-a, -b)], lev_s.at[i], lev_r.at[slot_of(-a, -b)])

    for i, (a, b) in enumerate(OFFSETS):
        beside(a, b, part_send.at[slot_of(a, b)], part_recv.at[slot_of(-a, -b)],
               part_s.at[i], part_r.at[slot_of(-a, -b)])

    stiff32 = stiff[...].astype(F32)
    for f, (a, b) in enumerate(FACES):
        stat_send[f, :primal, :] = phi[:, f * face:(f + 1) * face]
        stat_send[f, primal:, :] = jnp.broadcast_to(
            stiff32[:, f * face:(f + 1) * face], (16, face)).astype(BF16)
        to_face(f, stat_send.at[f], stat_recv.at[f ^ 1], stat_s.at[f], stat_r.at[f ^ 1],
                via_stat, via_r.at[4])

    for f in range(4):
        lane = lax.broadcasted_iota(jnp.int32, (1, face), 1)
        weight = jnp.where(lane < sizes[0, f], stiff32[:, f * face:(f + 1) * face], 0.0)
        for j in range(face // 128):
            square = jnp.broadcast_to(weight[:, j * 128:(j + 1) * 128], (128, 128))
            col[pl.ds(f * face + j * 128, 128), :] = square.T

    def across(column):
        return jnp.concatenate([column] * (width // 128), axis=1)

    def multiply(q):
        for f in range(4):
            inv_loads[4 * q + f].wait()

        def step(p, carry):
            one_face = pl.multiple_of(2 * p * face + q * quarter, quarter)
            next_face = pl.multiple_of((2 * p + 1) * face + q * quarter, quarter)
            here, there = pl.ds(one_face, quarter), pl.ds(next_face, quarter)
            value = dot(jnp.concatenate([inv[here, :], inv[there, :]], axis=0), masked[...])
            scale = jnp.concatenate([col[here, :], col[there, :]], axis=0)
            value = (value * across(scale)).astype(BF16)
            bulk_send[2 * p, q * quarter:(q + 1) * quarter, :] = value[:quarter]
            bulk_send[2 * p + 1, q * quarter:(q + 1) * quarter, :] = value[quarter:]
            return carry

        lax.fori_loop(0, 2, step, 0)

    eighth = face // 8

    def send_eighth(e):
        part = pl.ds(e * eighth, eighth)
        for f, (a, b) in enumerate(FACES):
            ends = (bulk_send.at[f, part], bulk_recv.at[f ^ 1, part],
                    bulk_s.at[4 * e + f], bulk_r.at[4 * e + (f ^ 1)])
            if e < 4:
                to_face(f, *ends, via_bulk.at[e], via_r.at[e])
            else:
                beside(a, b, *ends)

    def pass_eighth(e):
        part = pl.ds(e * eighth, eighth)
        pass_on(via_bulk.at[e], e, lambda slot: bulk_recv.at[slot, part],
                lambda slot: bulk_r.at[4 * e + slot])

    multiply(0)
    send_eighth(0)

    for a, b in OFFSETS:
        arrived(a, b, lev_ext.at[slot_of(a, b)], lev_s.at[0], lev_r.at[slot_of(a, b)])
    lev_all = lev_ext[...].reshape(9 * cdev, top_size)
    basis = dot(sel_t, lev_all, ((0,), (0,)), HIGHEST)
    basis_inv = dot(basis, topinv[...], ((1,), (1,)), HIGHEST)
    share = dot(basis_inv, partial[...], ((0,), (0,)), HIGHEST)
    red_send[...] = share.reshape(gy_count, piece, width).astype(BF16)

    for d in range(1, gy_count):
        to_group(gy_peer, d, red_send.at[lax.rem(y + d, gy_count)],
                 red_recv.at[d], red_s, red_r)

    total = part_send[slot_of(0, 0)].astype(F32)
    for a, b in OFFSETS:
        arrived(a, b, part_recv.at[slot_of(a, b)], part_s.at[0], part_r.at[slot_of(a, b)])
        total = total + part_recv[slot_of(a, b)].astype(F32)
    asm[...] = total.astype(BF16)

    def block_rows(index):
        return pl.ds(pl.multiple_of(index * cdev, cdev), cdev)

    def swap_peer(d):
        return (x, y + 1 - 2 * lax.rem(y, 2))

    own_rows = block_rows(y)
    for d in range(2, gy_count, 2):
        to_group(gy_peer, d, asm, blk.at[own_rows], asm_s, asm_r)
    to_group(swap_peer, 1, asm, blk.at[own_rows], asm_s, asm_r)
    blk[own_rows, :] = total.astype(BF16)

    send_eighth(1)
    multiply(1)
    send_eighth(2)

    total = red_send[y].astype(F32)
    for d in range(1, gy_count):
        group_arrived(gy_peer, d, red_recv.at[d], red_s, red_r)
        total = total + red_recv[d].astype(F32)
    run_send[...] = total.astype(BF16)
    for d in range(1, RUN):
        to_group(run_peer, d, run_send, run_recv.at[d], run_s, run_r)

    send_eighth(3)
    pass_on(via_stat, 4, lambda slot: stat_recv.at[slot], lambda slot: stat_r.at[slot])
    pass_eighth(0)
    for d in range(2, gy_count, 2):
        group_arrived(gy_peer, d, asm, asm_s, asm_r)
        passed = blk.at[block_rows(lax.rem(y - d + gy_count, gy_count))]
        to_group(swap_peer, d + 1, passed, passed, asm_s, asm_r)
    for d in range(1, gy_count, 2):
        group_arrived(swap_peer, d, asm, asm_s, asm_r)
    coarse = dot(block[...], blk[...].astype(F32), precision=HIGHEST)
    coarse_ext[slot_of(0, 0)] = coarse.astype(BF16)
    for i, (a, b) in enumerate(OFFSETS):
        beside(a, b, coarse_ext.at[slot_of(0, 0)], coarse_ext.at[slot_of(-a, -b)],
               coarse_s.at[i], coarse_r.at[slot_of(-a, -b)])
    multiply(2)
    send_eighth(4)
    pass_eighth(1)

    total = run_send[...].astype(F32)
    for d in range(1, RUN):
        group_arrived(run_peer, d, run_recv.at[d], run_s, run_r)
        total = total + run_recv[d].astype(F32)
    far_send[...] = total.astype(BF16)
    for d in range(1, far_count):
        to_group(far_peer, d, far_send, far_recv.at[d], far_s, far_r)
    pass_eighth(2)
    send_eighth(5)
    multiply(3)
    send_eighth(6)
    pass_eighth(3)

    low_send[:, width:] = jnp.concatenate(
        [basis, jnp.zeros((primal, low_send.shape[1] - width - top_size), F32)], axis=1
    ).astype(BF16)
    for f, (a, b) in enumerate(FACES):
        arrived(a, b, stat_recv.at[f], stat_s.at[f], stat_r.at[f])
        lane = lax.broadcasted_iota(jnp.int32, (1, face), 1)
        live = lane < sizes[0, f]
        own = stiff32[:, f * face:(f + 1) * face]
        other = stat_recv[f, primal:primal + 16, :].astype(F32)[:1]
        scale = jnp.where(live, 1.0 / (own + other), 0.0)
        for j in range(face // 128):
            square = jnp.broadcast_to(scale[:, j * 128:(j + 1) * 128], (128, 128))
            dencol[pl.ds(f * face + j * 128, 128), :] = square.T
        own_phi = (stat_send[f, :primal, :].astype(F32) * (own * scale)).astype(BF16)
        other_phi = (stat_recv[f, :primal, :].astype(F32) * (other * scale)).astype(BF16)
        phit[pl.ds(f * face, face), :2 * primal] = jnp.concatenate([own_phi, other_phi], axis=0).T

    total = far_send[...].astype(F32)
    for d in range(1, far_count):
        group_arrived(far_peer, d, far_recv.at[d], far_s, far_r)
        total = total + far_recv[d].astype(F32)
    piece_send[...] = total.astype(BF16)
    for d in range(1, gy_count):
        to_group(gy_peer, d, piece_send, top.at[y], top_s, top_r)
    top[y] = total.astype(BF16)
    send_eighth(7)

    for a, b in OFFSETS:
        arrived(a, b, coarse_ext.at[slot_of(a, b)], coarse_s.at[0], coarse_r.at[slot_of(a, b)])
    ext = coarse_ext[...].reshape(9 * cdev, width)
    low_send[:, :width] = dot(sel_t16, ext, ((0,), (0,))).astype(BF16)
    for f, (a, b) in enumerate(FACES):
        beside(a, b, low_send, low_recv.at[f ^ 1], low_s.at[f], low_r.at[f ^ 1])
    low_out[...] = low_send[...]

    for q in range(4):
        part = pl.ds(q * quarter, quarter)
        for f, (a, b) in enumerate(FACES):
            for e in (2 * q, 2 * q + 1):
                rows_e = pl.ds(e * eighth, eighth)
                arrived(a, b, bulk_recv.at[f, rows_e], bulk_s.at[4 * e + f], bulk_r.at[4 * e + f])
            summed = bulk_send[f, part, :].astype(F32) + bulk_recv[f, part, :].astype(F32)
            acc[quarter_rows(f, q), :] = summed * across(dencol[quarter_rows(f, q), :])
    for f, (a, b) in enumerate(FACES):
        arrived(a, b, low_recv.at[f], low_s.at[f], low_r.at[f])
        lowr_out[f] = low_recv[f]
    for d in range(1, gy_count):
        group_arrived(gy_peer, d, top.at[0], top_s, top_r)
    top_out[...] = top[...].astype(F32).reshape(top_size, width)
    for done in pending:
        done()


def finish_kernel(acc, phit, low, lowr, top, out_h, out, sem):
    top_size, width = top.shape
    primal = low.shape[0]
    face = acc.shape[0] // 4
    top16 = top[...].astype(BF16)

    def full(value):
        lifted = dot(value[:, width:width + top_size], top16)
        return (value[:, :width].astype(F32) + lifted).astype(BF16)

    own = full(low[...])
    copies = []
    for f in range(4):
        both = jnp.concatenate([own, full(lowr[f])], axis=0)
        here = pl.ds(f * face, face)
        out[here, :] = (acc[here, :] + dot(phit[here, :2 * primal], both)).astype(BF16)
        copy = pltpu.make_async_copy(out.at[here], out_h.at[here], sem.at[f])
        copy.start()
        copies.append(copy)
    for copy in copies:
        copy.wait()


def local(gx_count, gy_count, residual, local_inverse, primal_basis, row_stiffness,
          face_sizes, primal_slots, block_inverse, level_basis, top_inverse):
    rows, width = residual.shape[2:]
    face = rows // 4
    primal = primal_basis.shape[2]
    cdev, top_size = level_basis.shape[2:]
    block_size = block_inverse.shape[3]
    far_count = gx_count // RUN
    piece = top_size // gy_count
    low_width = width + 128
    vm = pltpu.VMEM
    dma = pltpu.SemaphoreType.DMA
    args = (residual[0, 0], local_inverse[0, 0], primal_basis[0, 0], row_stiffness[0],
            face_sizes[0], primal_slots[0], block_inverse[0, 0], level_basis[0, 0], top_inverse)
    args = [pltpu.with_memory_space_constraint(arg, pltpu.MemorySpace.HBM) for arg in args]
    halo = dma((9,))
    four = dma((4,))
    gys = dma((gy_count,))
    scratch = [
        vm((rows, width), BF16), vm((rows, rows), BF16), vm((primal, rows), BF16),
        vm((1, rows), BF16), pltpu.SMEM((1, 4), jnp.int32), vm((1, primal), jnp.int32),
        vm((cdev, block_size), F32), vm((cdev, top_size), F32), vm((top_size, top_size), F32),
        vm((rows, width), BF16), vm((rows, 128), F32), vm((rows, 128), F32),
        vm((9, cdev, top_size), F32), vm((primal, width), F32),
        vm((9, cdev, width), BF16), vm((9, cdev, width), BF16),
        vm((cdev, width), BF16), vm((block_size, width), BF16), vm((9, cdev, width), BF16),
        vm((4, primal + 16, face), BF16), vm((4, primal + 16, face), BF16),
        vm((4, face, width), BF16), vm((4, face, width), BF16),
        vm((primal, low_width), BF16), vm((4, primal, low_width), BF16),
        vm((gy_count, piece, width), BF16), vm((gy_count, piece, width), BF16),
        vm((piece, width), BF16), vm((RUN, piece, width), BF16),
        vm((piece, width), BF16), vm((far_count, piece, width), BF16),
        vm((piece, width), BF16), vm((gy_count, piece, width), BF16),
        vm((4, face // 8, width), BF16), vm((primal + 16, face), BF16),
        dma((11,)), dma((16,)),
        halo, halo, halo, halo, halo, halo,
        four, four, dma((32,)), dma((32,)), four, four,
        dma((5,)), dma((5,)), gys, gys, gys, gys, dma((RUN,)), dma((RUN,)), dma((far_count,)), dma((far_count,)),
        gys, gys,
    ]
    kept = (
        vm((rows, width), F32), vm((rows, 256), BF16), vm((primal, low_width), BF16),
        vm((4, primal, low_width), BF16), vm((top_size, width), F32))
    values = pl.pallas_call(
        functools.partial(apply_kernel, gx_count, gy_count),
        name="apply",
        out_shape=kept,
        in_specs=[pl.BlockSpec(memory_space=pltpu.MemorySpace.HBM)] * len(args),
        out_specs=[pl.BlockSpec(memory_space=pltpu.MemorySpace.VMEM)] * len(kept),
        scratch_shapes=scratch,
        compiler_params=pltpu.CompilerParams(
            collective_id=0, has_side_effects=True, vmem_limit_bytes=40 << 20),
    )(*args)
    out = pl.pallas_call(
        finish_kernel,
        name="finish",
        out_shape=jax.ShapeDtypeStruct((rows, width), BF16),
        in_specs=[pl.BlockSpec(memory_space=pltpu.MemorySpace.VMEM)] * len(kept),
        out_specs=pl.BlockSpec(memory_space=pl.ANY),
        scratch_shapes=[vm((rows, width), BF16), dma((4,))],
        compiler_params=pltpu.CompilerParams(vmem_limit_bytes=16 << 20),
    )(*values)
    return out[None, None]


def solution(mesh):
    in_specs = (
        P("gx", "gy", None, None),
        P("gx", "gy", None, None),
        P("gx", "gy", None, None),
        P("gx", "gy", None),
        P("gx", "gy", None),
        P("gx", "gy", None),
        P("gx", "gy", None, None),
        P("gx", "gy", None, None),
        P(),
    )
    out_specs = P("gx", "gy", None, None)
    body = functools.partial(local, mesh.shape["gx"], mesh.shape["gy"])
    return jax.shard_map(body, mesh=mesh, in_specs=in_specs, out_specs=out_specs, check_vma=False)
```

time: 64.4 us -> 51.3 us (0.80)
  Pallas kernels: 63.1 us -> 50.3 us
    pallas_call x1, Pallas kernels: 58.5 us -> 48.2 us  [local(): pl.pallas_call(functools.partial(apply_kernel, gx_count, gy_count), name=...]
    pallas_call x1, Pallas kernels: 4.6 us -> 2.09 us  [local(): pl.pallas_call(finish_kernel, name='finish', out_shape=jax.ShapeDtypeStru...]
where the time goes in v2:
time: 51.3 us; the launch traced here: 50.3 us
  Pallas kernels  50.3 us (98%)
    pallas_call x1, Pallas kernels, local(): pl.pallas_call(functools.partial(apply_kernel, gx_count, gy_count), name=...  48.2 us
    pallas_call x1, Pallas kernels, local(): pl.pallas_call(finish_kernel, name='finish', out_shape=jax.ShapeDtypeStru...  2.09 us

profile of v2, /device:TPU:1, one launch (start us, length us, event | category | flops | bytes accessed | tf_op | source)
XLA Modules:
  0.0 50.3 jit_solution(2786162689558662414)
XLA Ops:
  0.0 48.2 %apply.1 = (f32[2048,384]{1,0:T(8,128)S(1)}, bf16[2048,256]{1,0:T(8,128)(2,1)S(1)}, bf16[96,512]{1,0:T(8,128)(2,1)S(1)}, bf16[4,96,512]{2,1,0:T(8,128)(2,1)S(1)}, f32[64,384]{1,0:T(8,128)S(1)}) custom-call(bf16[2048,384]{1,0:T(8,128)(2,1)} %bitcast.10, bf16[2048,2048]{1,0:T(8,128)(2,1)} %bitcast.9, bf16[96,2048]{1,0:T(8,128)(2,1)} %bitcast.11, ...), custom_call_target="tpu_custom_call" | custom-call | tf_op jit(solution)/shard_map/apply/pallas_call | solution.py:464
  48.2 2.1 %finish.1 = bf16[2048,384]{1,0:T(8,128)(2,1)} custom-call(f32[2048,384]{1,0:T(8,128)S(1)} %get-tuple-element.10.acc, bf16[2048,256]{1,0:T(8,128)(2,1)S(1)} %get-tuple-element.11.phit, bf16[96,512]{1,0:T(8,128)(2,1)S(1)} %get-tuple-element.12.low, bf16[4,96,512]{2,1,0:T(8,128)(2,1)S(1)} %get-tuple-element.13.lowr, f32[64,384]{1,0:T(8,128)S(1)} %get-tuple-element.14.top), custom_call_target="tpu_custom_call" | custom-call | tf_op jit(solution)/shard_map/finish/pallas_call | solution.py:474

commit v3 on v2

--- a/solution.py
+++ b/solution.py
@@ -28,14 +28,14 @@
     gx_count,
     gy_count,
     res_h, inv_h, phi_h, stiff_h, sizes_h, slots_h, block_h, level_h, topinv_h,
-    acc, phit, low_out, lowr_out, top_out,
+    acc, phit, low_out, lowr_out, bas_out, basr_out, top_out,
     res, inv, phi, stiff, sizes, slots, block, level, topinv,
     masked, col, dencol, lev_ext, partial, part_send, part_recv, asm, blk, coarse_ext,
     stat_send, stat_recv, bulk_send, bulk_recv, low_send, low_recv,
     red_send, red_recv, run_send, run_recv, far_send, far_recv, piece_send, top,
-    via_bulk, via_stat, load_sem, inv_sem,
+    bas_send, bas_recv, via_bulk, via_stat, load_sem, inv_sem,
     lev_s, lev_r, part_s, part_r, coarse_s, coarse_r,
-    stat_s, stat_r, bulk_s, bulk_r, low_s, low_r,
+    stat_s, stat_r, bulk_s, bulk_r, low_s, low_r, bas_s, bas_r,
     via_s, via_r, red_s, red_r, asm_s, asm_r, run_s, run_r, far_s, far_r, top_s, top_r,
 ):
     x = lax.axis_index("gx")
@@ -181,6 +181,7 @@
         zero_outside(a, b, stat_recv.at[f])
         zero_outside(a, b, bulk_recv.at[f])
         zero_outside(a, b, low_recv.at[f])
+        zero_outside(a, b, bas_recv.at[f])
 
     for copy in loads:
         copy.wait()
@@ -189,6 +190,7 @@
     sel_t = jnp.where(slot_row == slot_iota, 1.0, 0.0).astype(F32)
     sel_t16 = sel_t.astype(BF16)
     lev_ext[slot_of(0, 0)] = level[...]
+    lift = dot(topinv[...], level[...], ((1,), (1,)), HIGHEST)
 
     for f in range(4):
         res_loads[f].wait()
@@ -208,11 +210,10 @@
         barrier, count_x * count_y - 1 + one(has_third) + gy_count - 1 + RUN - 1 + far_count - 1)
 
     for i, (a, b) in enumerate(OFFSETS):
-        beside(a, b, level, lev_ext.at[slot_of(-a, -b)], lev_s.at[i], lev_r.at[slot_of(-a, -b)])
-
-    for i, (a, b) in enumerate(OFFSETS):
         beside(a, b, part_send.at[slot_of(a, b)], part_recv.at[slot_of(-a, -b)],
                part_s.at[i], part_r.at[slot_of(-a, -b)])
+    for i, (a, b) in enumerate(OFFSETS):
+        beside(a, b, level, lev_ext.at[slot_of(-a, -b)], lev_s.at[i], lev_r.at[slot_of(-a, -b)])
 
     stiff32 = stiff[...].astype(F32)
     for f, (a, b) in enumerate(FACES):
@@ -268,23 +269,18 @@
 
     multiply(0)
     send_eighth(0)
-
-    for a, b in OFFSETS:
-        arrived(a, b, lev_ext.at[slot_of(a, b)], lev_s.at[0], lev_r.at[slot_of(a, b)])
-    lev_all = lev_ext[...].reshape(9 * cdev, top_size)
-    basis = dot(sel_t, lev_all, ((0,), (0,)), HIGHEST)
-    basis_inv = dot(basis, topinv[...], ((1,), (1,)), HIGHEST)
-    share = dot(basis_inv, partial[...], ((0,), (0,)), HIGHEST)
-    red_send[...] = share.reshape(gy_count, piece, width).astype(BF16)
-
-    for d in range(1, gy_count):
-        to_group(gy_peer, d, red_send.at[lax.rem(y + d, gy_count)],
-                 red_recv.at[d], red_s, red_r)
+    multiply(1)
 
     total = part_send[slot_of(0, 0)].astype(F32)
     for a, b in OFFSETS:
         arrived(a, b, part_recv.at[slot_of(a, b)], part_s.at[0], part_r.at[slot_of(a, b)])
         total = total + part_recv[slot_of(a, b)].astype(F32)
+    share = dot(lift, total, precision=HIGHEST)
+    red_send[...] = share.reshape(gy_count, piece, width).astype(BF16)
+
+    for d in range(1, gy_count):
+        to_group(gy_peer, d, red_send.at[lax.rem(y + d, gy_count)],
+                 red_recv.at[d], red_s, red_r)
     asm[...] = total.astype(BF16)
 
     def block_rows(index):
@@ -299,9 +295,17 @@
     to_group(swap_peer, 1, asm, blk.at[own_rows], asm_s, asm_r)
     blk[own_rows, :] = total.astype(BF16)
 
+    for a, b in OFFSETS:
+        arrived(a, b, lev_ext.at[slot_of(a, b)], lev_s.at[0], lev_r.at[slot_of(a, b)])
+    lev_all = lev_ext[...].reshape(9 * cdev, top_size)
+    basis = dot(sel_t, lev_all, ((0,), (0,)), HIGHEST)
+    bas_send[...] = jnp.concatenate(
+        [basis, jnp.zeros((primal, bas_send.shape[1] - top_size), F32)], axis=1).astype(BF16)
+    for f, (a, b) in enumerate(FACES):
+        beside(a, b, bas_send, bas_recv.at[f ^ 1], bas_s.at[f], bas_r.at[f ^ 1])
     send_eighth(1)
-    multiply(1)
     send_eighth(2)
+    multiply(2)
 
     total = red_send[y].astype(F32)
     for d in range(1, gy_count):
@@ -325,8 +329,9 @@
     for i, (a, b) in enumerate(OFFSETS):
         beside(a, b, coarse_ext.at[slot_of(0, 0)], coarse_ext.at[slot_of(-a, -b)],
                coarse_s.at[i], coarse_r.at[slot_of(-a, -b)])
-    multiply(2)
     send_eighth(4)
+    multiply(3)
+    send_eighth(5)
     pass_eighth(1)
 
     total = run_send[...].astype(F32)
@@ -336,17 +341,16 @@
     far_send[...] = total.astype(BF16)
     for d in range(1, far_count):
         to_group(far_peer, d, far_send, far_recv.at[d], far_s, far_r)
+    send_eighth(6)
     pass_eighth(2)
-    send_eighth(5)
-    multiply(3)
-    send_eighth(6)
     pass_eighth(3)
-
-    low_send[:, width:] = jnp.concatenate(
-        [basis, jnp.zeros((primal, low_send.shape[1] - width - top_size), F32)], axis=1
-    ).astype(BF16)
+    send_eighth(7)
+
+    bas_out[...] = bas_send[...]
     for f, (a, b) in enumerate(FACES):
         arrived(a, b, stat_recv.at[f], stat_s.at[f], stat_r.at[f])
+        arrived(a, b, bas_recv.at[f], bas_s.at[f], bas_r.at[f])
+        basr_out[f] = bas_recv[f]
         lane = lax.broadcasted_iota(jnp.int32, (1, face), 1)
         live = lane < sizes[0, f]
         own = stiff32[:, f * face:(f + 1) * face]
@@ -359,6 +363,12 @@
         other_phi = (stat_recv[f, :primal, :].astype(F32) * (other * scale)).astype(BF16)
         phit[pl.ds(f * face, face), :2 * primal] = jnp.concatenate([own_phi, other_phi], axis=0).T
 
+    for a, b in OFFSETS:
+        arrived(a, b, coarse_ext.at[slot_of(a, b)], coarse_s.at[0], coarse_r.at[slot_of(a, b)])
+    ext = coarse_ext[...].reshape(9 * cdev, width)
+    low_send[...] = dot(sel_t16, ext, ((0,), (0,))).astype(BF16)
+    for f, (a, b) in enumerate(FACES):
+        beside(a, b, low_send, low_recv.at[f ^ 1], low_s.at[f], low_r.at[f ^ 1])
     total = far_send[...].astype(F32)
     for d in range(1, far_count):
         group_arrived(far_peer, d, far_recv.at[d], far_s, far_r)
@@ -367,14 +377,7 @@
     for d in range(1, gy_count):
         to_group(gy_peer, d, piece_send, top.at[y], top_s, top_r)
     top[y] = total.astype(BF16)
-    send_eighth(7)
-
-    for a, b in OFFSETS:
-        arrived(a, b, coarse_ext.at[slot_of(a, b)], coarse_s.at[0], coarse_r.at[slot_of(a, b)])
-    ext = coarse_ext[...].reshape(9 * cdev, width)
-    low_send[:, :width] = dot(sel_t16, ext, ((0,), (0,))).astype(BF16)
-    for f, (a, b) in enumerate(FACES):
-        beside(a, b, low_send, low_recv.at[f ^ 1], low_s.at[f], low_r.at[f ^ 1])
+
     low_out[...] = low_send[...]
 
     for q in range(4):
@@ -385,30 +388,29 @@
                 arrived(a, b, bulk_recv.at[f, rows_e], bulk_s.at[4 * e + f], bulk_r.at[4 * e + f])
             summed = bulk_send[f, part, :].astype(F32) + bulk_recv[f, part, :].astype(F32)
             acc[quarter_rows(f, q), :] = summed * across(dencol[quarter_rows(f, q), :])
+    for done in pending:
+        done()
     for f, (a, b) in enumerate(FACES):
         arrived(a, b, low_recv.at[f], low_s.at[f], low_r.at[f])
         lowr_out[f] = low_recv[f]
     for d in range(1, gy_count):
         group_arrived(gy_peer, d, top.at[0], top_s, top_r)
     top_out[...] = top[...].astype(F32).reshape(top_size, width)
-    for done in pending:
-        done()
-
-
-def finish_kernel(acc, phit, low, lowr, top, out_h, out, sem):
-    top_size, width = top.shape
+
+
+def finish_kernel(acc, phit, low, lowr, bas, basr, top, out_h, out, sem):
+    top_size = top.shape[0]
     primal = low.shape[0]
     face = acc.shape[0] // 4
     top16 = top[...].astype(BF16)
 
-    def full(value):
-        lifted = dot(value[:, width:width + top_size], top16)
-        return (value[:, :width].astype(F32) + lifted).astype(BF16)
-
-    own = full(low[...])
+    def full(value, basis):
+        return (value.astype(F32) + dot(basis[:, :top_size], top16)).astype(BF16)
+
+    own = full(low[...], bas[...])
     copies = []
     for f in range(4):
-        both = jnp.concatenate([own, full(lowr[f])], axis=0)
+        both = jnp.concatenate([own, full(lowr[f], basr[f])], axis=0)
         here = pl.ds(f * face, face)
         out[here, :] = (acc[here, :] + dot(phit[here, :2 * primal], both)).astype(BF16)
         copy = pltpu.make_async_copy(out.at[here], out_h.at[here], sem.at[f])
@@ -427,7 +429,6 @@
     block_size = block_inverse.shape[3]
     far_count = gx_count // RUN
     piece = top_size // gy_count
-    low_width = width + 128
     vm = pltpu.VMEM
     dma = pltpu.SemaphoreType.DMA
     args = (residual[0, 0], local_inverse[0, 0], primal_basis[0, 0], row_stiffness[0],
@@ -446,21 +447,23 @@
         vm((cdev, width), BF16), vm((block_size, width), BF16), vm((9, cdev, width), BF16),
         vm((4, primal + 16, face), BF16), vm((4, primal + 16, face), BF16),
         vm((4, face, width), BF16), vm((4, face, width), BF16),
-        vm((primal, low_width), BF16), vm((4, primal, low_width), BF16),
+        vm((primal, width), BF16), vm((4, primal, width), BF16),
         vm((gy_count, piece, width), BF16), vm((gy_count, piece, width), BF16),
         vm((piece, width), BF16), vm((RUN, piece, width), BF16),
         vm((piece, width), BF16), vm((far_count, piece, width), BF16),
         vm((piece, width), BF16), vm((gy_count, piece, width), BF16),
+        vm((primal, 128), BF16), vm((4, primal, 128), BF16),
         vm((4, face // 8, width), BF16), vm((primal + 16, face), BF16),
         dma((11,)), dma((16,)),
         halo, halo, halo, halo, halo, halo,
-        four, four, dma((32,)), dma((32,)), four, four,
+        four, four, dma((32,)), dma((32,)), four, four, four, four,
         dma((5,)), dma((5,)), gys, gys, gys, gys, dma((RUN,)), dma((RUN,)), dma((far_count,)), dma((far_count,)),
         gys, gys,
     ]
     kept = (
-        vm((rows, width), F32), vm((rows, 256), BF16), vm((primal, low_width), BF16),
-        vm((4, primal, low_width), BF16), vm((top_size, width), F32))
+        vm((rows, width), F32), vm((rows, 256), BF16), vm((primal, width), BF16),
+        vm((4, primal, width), BF16), vm((primal, 128), BF16), vm((4, primal, 128), BF16),
+        vm((top_size, width), F32))
     values = pl.pallas_call(
         functools.partial(apply_kernel, gx_count, gy_count),
         name="apply",

time: 51.3 us -> 49.6 us (0.967); the launches traced: 50.3 us -> 49.5 us
  Pallas kernels: 50.3 us -> 49.5 us
    pallas_call x1, Pallas kernels: 48.2 us -> 47.4 us  [local(): pl.pallas_call(functools.partial(apply_kernel, gx_count, gy_count), name=...]
where the time goes in v3:
time: 49.6 us; the launch traced here: 49.5 us
  Pallas kernels  49.5 us (100%)
    pallas_call x1, Pallas kernels, local(): pl.pallas_call(functools.partial(apply_kernel, gx_count, gy_count), name=...  47.4 us
    pallas_call x1, Pallas kernels, local(): pl.pallas_call(finish_kernel, name='finish', out_shape=jax.ShapeDtypeStru...  2.1 us

profile of v3, /device:TPU:1, one launch (start us, length us, event | category | flops | bytes accessed | tf_op | source)
XLA Modules:
  0.0 49.5 jit_solution(15254505886453955716)
XLA Ops:
  0.0 47.4 %apply.1 = (f32[2048,384]{1,0:T(8,128)S(1)}, bf16[2048,256]{1,0:T(8,128)(2,1)S(1)}, bf16[96,384]{1,0:T(8,128)(2,1)S(1)}, bf16[4,96,384]{2,1,0:T(8,128)(2,1)S(1)}...) custom-call(bf16[2048,384]{1,0:T(8,128)(2,1)} %bitcast.10, ...), custom_call_target="tpu_custom_call" | custom-call | tf_op jit(solution)/shard_map/apply/pallas_call | solution.py:467
  47.4 2.1 %finish.1 = bf16[2048,384]{1,0:T(8,128)(2,1)} custom-call(f32[2048,384]{1,0:T(8,128)S(1)} %get-tuple-element.12.acc, bf16[2048,256]{1,0:T(8,128)(2,1)S(1)} %get-tuple-element.13.phit, bf16[96,384]{1,0:T(8,128)(2,1)S(1)} %get-tuple-element.14.low, bf16[4,96,384]{2,1,0:T(8,128)(2,1)S(1)} %get-tuple-element.15.lowr, bf16[96,128]{1,0:T(8,128)(2,1)S(1)} %get-tuple-element.16.bas, ...), custom_call_target="tpu_custom_call" | custom-call | tf_op jit(solution)/shard_map/finish/pallas_call | solution.py:477

commit v4 on v3

--- a/solution.py
+++ b/solution.py
@@ -190,6 +190,8 @@
     sel_t = jnp.where(slot_row == slot_iota, 1.0, 0.0).astype(F32)
     sel_t16 = sel_t.astype(BF16)
     lev_ext[slot_of(0, 0)] = level[...]
+    block_high = block[...].astype(BF16)
+    block_low = (block[...] - block_high.astype(F32)).astype(BF16)
     lift = dot(topinv[...], level[...], ((1,), (1,)), HIGHEST)
 
     for f in range(4):
@@ -324,7 +326,7 @@
         to_group(swap_peer, d + 1, passed, passed, asm_s, asm_r)
     for d in range(1, gy_count, 2):
         group_arrived(swap_peer, d, asm, asm_s, asm_r)
-    coarse = dot(block[...], blk[...].astype(F32), precision=HIGHEST)
+    coarse = dot(block_high, blk[...]) + dot(block_low, blk[...])
     coarse_ext[slot_of(0, 0)] = coarse.astype(BF16)
     for i, (a, b) in enumerate(OFFSETS):
         beside(a, b, coarse_ext.at[slot_of(0, 0)], coarse_ext.at[slot_of(-a, -b)],

time: 49.6 us -> 49.6 us (level)
  no operation moved by 1% of the time
where the time goes in v4:
time: 49.6 us
  Pallas kernels  49.6 us (100%)
    pallas_call x1, Pallas kernels, local(): pl.pallas_call(functools.partial(apply_kernel, gx_count, gy_count), name=...  47.5 us
    pallas_call x1, Pallas kernels, local(): pl.pallas_call(finish_kernel, name='finish', out_shape=jax.ShapeDtypeStru...  2.1 us

profile of v4, /device:TPU:1, one launch (start us, length us, event | category | flops | bytes accessed | tf_op | source)
XLA Modules:
  0.0 49.6 jit_solution(4501305043929899642)
XLA Ops:
  0.0 47.5 %apply.1 = (f32[2048,384]{1,0:T(8,128)S(1)}, bf16[2048,256]{1,0:T(8,128)(2,1)S(1)}, bf16[96,384]{1,0:T(8,128)(2,1)S(1)}, bf16[4,96,384]{2,1,0:T(8,128)(2,1)S(1)}...) custom-call(bf16[2048,384]{1,0:T(8,128)(2,1)} %bitcast.10, ...), custom_call_target="tpu_custom_call" | custom-call | tf_op jit(solution)/shard_map/apply/pallas_call | solution.py:469
  47.5 2.1 %finish.1 = bf16[2048,384]{1,0:T(8,128)(2,1)} custom-call(f32[2048,384]{1,0:T(8,128)S(1)} %get-tuple-element.12.acc, bf16[2048,256]{1,0:T(8,128)(2,1)S(1)} %get-tuple-element.13.phit, bf16[96,384]{1,0:T(8,128)(2,1)S(1)} %get-tuple-element.14.low, bf16[4,96,384]{2,1,0:T(8,128)(2,1)S(1)} %get-tuple-element.15.lowr, bf16[96,128]{1,0:T(8,128)(2,1)S(1)} %get-tuple-element.16.bas, ...), custom_call_target="tpu_custom_call" | custom-call | tf_op jit(solution)/shard_map/finish/pallas_call | solution.py:479
